TPU v7x, 32 devices: a whole 2x2x4 slice. The times are simulated.
32 devices in a mesh: section: 8 (over z, x), sp: 4 (over y, core).
Axes of the slice: x: 2, y: 2, z: 4, core: 2. Of those that a mesh axis runs over, the one named last changes fastest.
Arguments:
- slots: bfloat16 [8, 64, 3072], P('section', 'sp'), may hold values from -6 to 6
- patch_of_slot: int32 [8], replicated, may hold values from 0 to 7, each once
- step_of_slot: int32 [8], replicated, may hold values from 0 to 26
- modulation: bfloat16 [8, 28, 3, 3072], P('section'), may hold values from -4 to 4
- w_qkv: bfloat16 [8, 3072, 3, 2048], P('section', None, None, 'sp'), may hold values from -0.109375 to 0.109375
- qk_scale: bfloat16 [8, 2, 128], P('section'), may hold values from 0.25 to 4
- w_mlp_in: bfloat16 [8, 3072, 6144], P('section', None, 'sp'), may hold values from -0.109375 to 0.109375
- w_attn_out: bfloat16 [8, 2048, 3072], P('section', 'sp'), may hold values from -0.125 to 0.125
- w_mlp_out: bfloat16 [8, 6144, 3072], P('section', 'sp'), may hold values from -0.078125 to 0.078125
- kv_cache: bfloat16 [8, 2, 512, 2048], P('section', None, None, 'sp'), may hold values from -130 to 130
Outputs:
- slots_out: bfloat16 [8, 64, 3072], P('section', 'sp')
- kv_cache_out: bfloat16 [8, 2, 512, 2048], P('section', None, None, 'sp')
Inputs may be any that keep to these rules, and one draw needn't show every extreme that they name: `patch_of_slot`: each patch id names exactly one slot.
All inputs are finite; a program needn't handle non-finite values.
Results may differ from a plain program's by a relative error of at most 0.012.
The roundings to bfloat16 on the way count: a program that leaves them out, or rounds other values in their place, can miss the bound.
Values may be sent and summed in bfloat16 or wider, within the bound.
A program may use at most 128 MiB of HBM per device.

v0:
```python
import math
import jax
import jax.numpy as jnp
from jax import lax
from jax.sharding import PartitionSpec as P

HD = 128
ROUNDS = 2


def shifted_2(x, axis, by):
    length = lax.axis_size(axis)
    return lax.ppermute(x, axis, [(i, (i + by) % length) for i in range(length)])


def slot_labels(patch_of_slot, step_of_slot, section_id, sections, round_id):
    anchor = section_id - round_id
    wrapped = (anchor < 0).astype(jnp.int32)
    anchor = anchor + wrapped * sections
    patch_id = lax.dynamic_index_in_dim(patch_of_slot, anchor, 0, keepdims=False)
    timestep = lax.dynamic_index_in_dim(step_of_slot, anchor, 0, keepdims=False) + wrapped
    return (patch_id, timestep)


def modulate(slot, table, timestep):
    factors = lax.dynamic_index_in_dim(table, timestep, 0, keepdims=False).astype(jnp.float32)
    wide = slot.astype(jnp.float32)
    center = wide - jnp.mean(wide, axis=-1, keepdims=True)
    spread = jnp.mean(center * center, axis=-1, keepdims=True)
    normed = (center * lax.rsqrt(spread + 1e-06) * (1.0 + factors[1]) + factors[0]).astype(
        jnp.bfloat16
    )
    return (normed, factors[2])


def head_norm(part, gain):
    rows = part.shape[0]
    wide = part.astype(jnp.float32).reshape(rows, -1, HD)
    power = jnp.mean(wide * wide, axis=-1, keepdims=True)
    normed = wide * lax.rsqrt(power + 1e-06) * gain.astype(jnp.float32)
    return normed.astype(jnp.bfloat16).reshape(rows, -1)


def mix(normed, patch_id, keys, values, qkv_weight, norm_gain, inner_weight):
    patch_rows = normed.shape[0]
    projected = jnp.einsum(
        "rd,dce->rce", normed, qkv_weight, preferred_element_type=jnp.float32
    ).astype(jnp.bfloat16)
    query_normed = head_norm(projected[:, 0], norm_gain[0])
    key_normed = head_norm(projected[:, 1], norm_gain[1])
    first_row = patch_id * patch_rows
    keys = lax.dynamic_update_slice_in_dim(keys, key_normed, first_row, 0)
    values = lax.dynamic_update_slice_in_dim(values, projected[:, 2], first_row, 0)
    local_heads = qkv_weight.shape[2] // HD
    queries = query_normed.reshape(patch_rows, local_heads, HD)
    key_heads = keys.reshape(keys.shape[0], local_heads, HD)
    value_heads = values.reshape(values.shape[0], local_heads, HD)
    scores = jnp.einsum(
        "rhd,thd->hrt", queries, key_heads, preferred_element_type=jnp.float32
    ) / math.sqrt(HD)
    shifted = jnp.exp(scores - jnp.max(scores, axis=-1, keepdims=True))
    weights = (shifted / jnp.sum(shifted, axis=-1, keepdims=True)).astype(jnp.bfloat16)
    attention = jnp.einsum(
        "hrt,thd->rhd", weights, value_heads, preferred_element_type=jnp.float32
    ).astype(jnp.bfloat16)
    attention = attention.reshape(patch_rows, local_heads * HD)
    activity = jax.nn.gelu(
        jnp.dot(normed, inner_weight, preferred_element_type=jnp.float32), approximate=True
    ).astype(jnp.bfloat16)
    return (attention, activity, keys, values)


def shards(
    slots,
    patch_of_slot,
    step_of_slot,
    modulation,
    w_qkv,
    qk_scale,
    w_mlp_in,
    w_attn_out,
    w_mlp_out,
    kv_cache,
):
    sections = lax.axis_size("section")
    section_id = lax.axis_index("section")
    table = modulation[0]
    qkv_weight = w_qkv[0]
    norm_gain = qk_scale[0]
    inner_weight = w_mlp_in[0]
    attention_weight = w_attn_out[0]
    outer_weight = w_mlp_out[0]
    keys = kv_cache[0, 0]
    values = kv_cache[0, 1]
    current = slots[0]
    for round_id in range(ROUNDS):
        patch_id, timestep = slot_labels(
            patch_of_slot, step_of_slot, section_id, sections, round_id
        )
        normed, gate = modulate(current, table, timestep)
        gathered = lax.all_gather(normed, "sp", axis=0, tiled=True)
        attention, activity, keys, values = mix(
            gathered, patch_id, keys, values, qkv_weight, norm_gain, inner_weight
        )
        summed = lax.psum_scatter(
            jnp.dot(attention, attention_weight, preferred_element_type=jnp.float32)
            + jnp.dot(activity, outer_weight, preferred_element_type=jnp.float32),
            "sp",
            scatter_dimension=0,
            tiled=True,
        )
        current = (current.astype(jnp.float32) + gate * summed).astype(jnp.bfloat16)
        current = shifted_2(current, "section", 1)
    return (current[None], jnp.stack([keys, values])[None])


def solution(mesh):
    return jax.shard_map(
        shards,
        mesh=mesh,
        in_specs=(
            P("section", "sp", None),
            P(),
            P(),
            P("section", None, None, None),
            P("section", None, None, "sp"),
            P("section", None, None),
            P("section", None, "sp"),
            P("section", "sp", None),
            P("section", "sp", None),
            P("section", None, None, "sp"),
        ),
        out_specs=(P("section", "sp", None), P("section", None, None, "sp")),
        check_vma=False,
    )
```

profile of v0, /device:TPU:0, one launch (start us, length us, event | category | flops | bytes accessed | tf_op | source)
XLA Modules:
  0.0 167.5 jit_solution(4243457292436387553)
XLA Ops:
  7.2 1.5 fusion.120
  10.0 1.1 dynamic-slice_convert_fusion
  11.1 1.0 convert_reduce_fusion.1
  12.1 1.1 fusion.78
  13.3 1.0 fusion.81
  14.3 8.0 %all_gather.6 = bf16[64,3072]{1,0:T(8,128)(2,1)S(1)} all-gather(bf16[16,3072]{1,0:T(8,128)(2,1)S(1)} %fusion.81), channel_id=1, replica_groups=mesh['section'=8,'sp'=4] {'sp'}, dimensions={0}, use_global_device_ids=true | all-gather | bytes 491520 | tf_op jit(solution)/shard_map/all_gather | solution.py:101
  23.0 5.4 %fusion.20 = bf16[64,3,512]{2,0,1:T(8,128)(2,1)S(1)} fusion(bf16[1,3072,3,512]{3,1,2,0:T(8,128)(2,1)} %param.14, bf16[64,3072]{1,0:T(8,128)(2,1)S(1)} %all_gather.6), kind=kOutput, calls=%fused_computation.24 | convolution fusion | flops 604078080 | bytes 10027008 | tf_op jit(solution)/shard_map/rd,dce->rce/dot_general | solution.py:46
  32.7 1.3 bitcast_convert_fusion.1
  34.6 2.3 %slice_bitcast_fusion = (bf16[512,512]{1,0:T(8,128)(2,1)}, bf16[512,512]{1,0:T(8,128)(2,1)}) fusion(bf16[1,2,512,512]{3,2,1,0:T(8,128)(2,1)} %param.19), kind=kLoop, calls=%fused_computation.43 | loop fusion | bytes 2097152 | tf_op jit(solution)/shard_map/squeeze | solution.py:93
  39.6 1.3 fusion.99
  41.0 1.3 convolution_multiply_fusion.1
  43.3 2.0 %fusion.26 = bf16[4,8,8,128]{3,2,1,0:T(8,128)(2,1)S(1)} fusion(f32[4,64]{1,0:T(4,128)S(1)} %fusion.122, f32[4,64,512]{2,1,0:T(8,128)} %copy-done.3, bf16[512,512]{1,0:T(8,128)(2,1)} %get-tuple-element.9), kind=kOutput, calls=%fused_computation.28 | convolution fusion | flops 33981184 | bytes 1115136 | tf_op jit(solution)/shard_map/hrt,thd->rhd/dot_general | solution.py:63
  45.4 10.8 %fusion.4 = f32[64,3072]{1,0:T(8,128)} fusion(bf16[1,1536,3072]{2,1,0:T(8,128)(2,1)} %param.18, bf16[64,3072]{1,0:T(8,128)(2,1)} %copy-done.1, bf16[1,3072,1536]{2,1,0:T(8,128)(2,1)} %param.16), kind=kOutput, calls=%fused_computation.4 | convolution fusion | flops 1208844288 | bytes 20054016 | tf_op jit(solution)/shard_map/dot_general | solution.py:107
  56.2 2.7 %convolution_add_fusion.1 = f32[64,3072]{1,0:T(8,128)} fusion(f32[64,3072]{1,0:T(8,128)} %fusion.4, bf16[1,512,3072]{2,1,0:T(8,128)(2,1)S(1)} %copy-done, bf16[4,8,8,128]{3,2,1,0:T(8,128)(2,1)S(1)} %fusion.26), kind=kOutput, calls=%fused_computation.15 | convolution fusion | flops 201523200 | bytes 4784128 | tf_op jit(solution)/shard_map/dot_general | solution.py:106
  58.9 24.2 %reduce-scatter.3.cloned.1.call-done = f32[16,3072]{1,0:T(8,128)} async-done(((f32[64,3072]{1,0:T(8,128)}), f32[16,3072]{1,0:T(8,128)}) %reduce-scatter.3.cloned.1.call-update) | async-done | bytes 196624 | tf_op jit(solution)/shard_map/reduce_scatter | solution.py:105
  84.1 1.5 collective-permute-start
  86.3 5.2 %collective-permute-done = bf16[16,3072]{1,0:T(8,128)(2,1)S(1)} collective-permute-done((bf16[16,3072]{1,0:T(8,128)(2,1)S(1)}, bf16[16,3072]{1,0:T(8,128)(2,1)S(1)}, u32[]{:S(2)}, u32[]{:S(2)}) %collective-permute-start) | collective-permute-done | bytes 98336 | tf_op jit(solution)/shard_map/ppermute | solution.py:13
  92.0 6.3 %all_gather.7 = bf16[64,3072]{1,0:T(8,128)(2,1)S(1)} all-gather(bf16[16,3072]{1,0:T(8,128)(2,1)S(1)} %fusion.77), channel_id=1, replica_groups=mesh['section'=8,'sp'=4] {'sp'}, dimensions={0}, use_global_device_ids=true | all-gather | bytes 491520 | tf_op jit(solution)/shard_map/all_gather | solution.py:101
  99.0 5.4 %fusion.23 = bf16[64,3,512]{2,0,1:T(8,128)(2,1)S(1)} fusion(bf16[1,3072,3,512]{3,1,2,0:T(8,128)(2,1)} %param.14, bf16[64,3072]{1,0:T(8,128)(2,1)S(1)} %all_gather.7), kind=kOutput, calls=%fused_computation.25 | convolution fusion | flops 604078080 | bytes 10027008 | tf_op jit(solution)/shard_map/rd,dce->rce/dot_general | solution.py:46
  105.8 10.8 %fusion.2 = f32[64,3072]{1,0:T(8,128)} fusion(bf16[1,1536,3072]{2,1,0:T(8,128)(2,1)} %param.18, bf16[64,3072]{1,0:T(8,128)(2,1)} %copy-done.2, bf16[1,3072,1536]{2,1,0:T(8,128)(2,1)} %param.16), kind=kOutput, calls=%fused_computation.2 | convolution fusion | flops 1208844288 | bytes 20054016 | tf_op jit(solution)/shard_map/dot_general | solution.py:107
  116.5 1.6 mul.270
  118.1 1.0 reduce_sum.98
  119.2 1.6 reshape.151
  120.8 1.0 multiply_reduce_fusion
  121.9 1.0 multiply_convert_fusion
  123.7 1.3 convolution_multiply_fusion
  126.1 1.9 %fusion.27 = bf16[4,8,8,128]{3,2,1,0:T(8,128)(2,1)S(1)} fusion(f32[4,64]{1,0:T(4,128)S(1)} %fusion.123, f32[4,64,512]{2,1,0:T(8,128)} %copy-done.4, bf16[512,512]{1,0:T(8,128)(2,1)} %get-tuple-element.7), kind=kOutput, calls=%fused_computation.29 | convolution fusion | flops 33981184 | bytes 1115136 | tf_op jit(solution)/shard_map/hrt,thd->rhd/dot_general | solution.py:63
  128.1 2.7 %convolution_add_fusion = f32[64,3072]{1,0:T(8,128)} fusion(f32[64,3072]{1,0:T(8,128)} %fusion.2, bf16[1,512,3072]{2,1,0:T(8,128)(2,1)S(1)} %copy-done, bf16[4,8,8,128]{3,2,1,0:T(8,128)(2,1)S(1)} %fusion.27), kind=kOutput, calls=%fused_computation.14 | convolution fusion | flops 201523200 | bytes 4784128 | tf_op jit(solution)/shard_map/dot_general | solution.py:106
  130.8 21.0 %reduce-scatter.5.cloned.1.call-done = f32[16,3072]{1,0:T(8,128)} async-done(((f32[64,3072]{1,0:T(8,128)}), f32[16,3072]{1,0:T(8,128)}) %reduce-scatter.5.cloned.1.call-update) | async-done | bytes 196624 | tf_op jit(solution)/shard_map/reduce_scatter | solution.py:105
  152.7 1.5 collective-permute-start.1
  154.2 2.3 %maximum_bitcast_fusion = bf16[1,2,512,512]{3,2,1,0:T(8,128)(2,1)} fusion(bf16[1,512,512]{2,1,0:T(8,128)(2,1)} %bitcast.182, bf16[1,512,512]{2,1,0:T(8,128)(2,1)} %bitcast.181), kind=kLoop, calls=%fused_computation.30 | loop fusion | flops 524288 | bytes 2097152 | tf_op jit(solution)/shard_map/broadcast_in_dim | solution.py:114
  156.5 3.6 %collective-permute-done.1 = bf16[16,3072]{1,0:T(8,128)(2,1)S(1)} collective-permute-done((bf16[16,3072]{1,0:T(8,128)(2,1)S(1)}, bf16[16,3072]{1,0:T(8,128)(2,1)S(1)}, u32[]{:S(2)}, u32[]{:S(2)}) %collective-permute-start.1) | collective-permute-done | bytes 98336 | tf_op jit(solution)/shard_map/ppermute | solution.py:13
  (51 shorter events, 16.0 us)
Async XLA Ops:
  7.2 49.0 %copy-start = (bf16[1,512,3072]{2,1,0:T(8,128)(2,1)S(1)}, bf16[1,512,3072]{2,1,0:T(8,128)(2,1)}, u32[]{:S(2)}) copy-start(bf16[1,512,3072]{2,1,0:T(8,128)(2,1)} %param.17) | copy-start | bytes 9437188
  7.2 76.0 %reduce-scatter.3.cloned.1.call-start = ((), (), s32[]{:S(2)}) async-start(), calls=%async_computation.2 | async-start | bytes 983040 | tf_op jit(solution)/shard_map/reduce_scatter | solution.py:105
  22.2 0.7 copy-start.1
  42.3 0.8 copy-start.3
  45.4 37.8 %copy-start.5 = (bf16[1,16,3072]{2,1,0:T(8,128)(2,1)S(1)}, bf16[1,16,3072]{2,1,0:T(8,128)(2,1)}, u32[]{:S(2)}) copy-start(bf16[1,16,3072]{2,1,0:T(8,128)(2,1)} %param.10) | copy-start | bytes 294916
  58.9 92.9 %reduce-scatter.5.cloned.1.call-start = ((), (), s32[]{:S(2)}) async-start(), calls=%async_computation.3 | async-start | bytes 983040 | tf_op jit(solution)/shard_map/reduce_scatter | solution.py:105
  84.1 7.4 %collective-permute-start = (bf16[16,3072]{1,0:T(8,128)(2,1)S(1)}, bf16[16,3072]{1,0:T(8,128)(2,1)S(1)}, u32[]{:S(2)}, u32[]{:S(2)}) collective-permute-start(bf16[16,3072]{1,0:T(8,128)(2,1)S(1)} %fusion.82), channel_id=1, source_target_pairs={{0,4},{4,8},{8,12},{12,16},{16,20},{20,24},{24,28},{28,0},{1,5},{5... | collective-permute-start | bytes 294920 | tf_op jit(solution)/shard_map/ppermute | solution.py:13
  98.3 0.7 copy-start.2
  105.8 16.1 %copy-start.7 = (f32[128]{0:T(128)S(1)}, f32[128]{0:T(128)}, u32[]{:S(2)}) copy-start(f32[128]{0:T(128)} %get-tuple-element.20) | copy-start | bytes 1540
  105.8 17.3 %copy-start.6 = (f32[512]{0:T(512)S(1)}, f32[512]{0:T(512)}, u32[]{:S(2)}) copy-start(f32[512]{0:T(512)} %broadcast_bitcast_fusion) | copy-start | bytes 6148
  125.1 0.8 copy-start.4
  152.7 7.4 %collective-permute-start.1 = (bf16[16,3072]{1,0:T(8,128)(2,1)S(1)}, bf16[16,3072]{1,0:T(8,128)(2,1)S(1)}, u32[]{:S(2)}, u32[]{:S(2)}) collective-permute-start(bf16[16,3072]{1,0:T(8,128)(2,1)S(1)} %fusion.83), channel_id=1, source_target_pairs={{0,4},{4,8},{8,12},{12,16},{16,20},{20,24},{24,28},{28,0},{1,5},{5... | collective-permute-start | bytes 294920 | tf_op jit(solution)/shard_map/ppermute | solution.py:13
Sparse Core Ops, SparseCore 0:
  59.0 24.1 reduce-scatter.2
  130.9 20.7 reduce-scatter.4
where the time goes:
time: 169 us; the launch traced here: 168 us
  waiting for transfers between devices  54 us (32%)
  matrix products  44.3 us (26%)
  other arithmetic  21.6 us (13%)
  between operations  16.8 us (10%)
  blocking collectives  14.3 us (8%)
  local copies, waits for them, and re-layouts  13.4 us (8%)
  starting transfers between devices  3.15 us (2%)
    reduce_scatter x2, waiting for transfers between devices, shards(): lax.psum_scatter(jnp.dot(attention, attention_weight, preferred_element_t...  45.2 us
    dot_general x2, matrix products, shards(): jnp.dot(activity, outer_weight, preferred_element_type=jnp.float32)  21.6 us
    all_gather x2, blocking collectives, shards(): gathered = lax.all_gather(normed, 'sp', axis=0, tiled=True)  14.3 us
    dot_general x2, matrix products, mix(): jnp.einsum('rd,dce->rce', normed, qkv_weight, preferred_element_type=jnp....  10.8 us
    ppermute x2, waiting for transfers between devices, shifted_2(): lax.ppermute(x, axis, [(i, (i + by) % length) for i in range(length)])  8.74 us
    dot_general x2, matrix products, shards(): jnp.dot(attention, attention_weight, preferred_element_type=jnp.float32)  5.36 us
    dot_general x2, matrix products, mix(): jnp.einsum('hrt,thd->rhd', weights, value_heads, preferred_element_type=j...  3.95 us
    unnamed x17, local copies, waits for them, and re-layouts  3.75 us
  transfers between devices with their start and end apart: 4, of which 4 were waited for; matrix products, arithmetic and copies ran while one was open for 1% of the time, Pallas kernels for 0%

commit v1 on v0

--- a/solution.py
+++ b/solution.py
@@ -98,7 +98,14 @@
             patch_of_slot, step_of_slot, section_id, sections, round_id
         )
         normed, gate = modulate(current, table, timestep)
-        gathered = lax.all_gather(normed, "sp", axis=0, tiled=True)
+        ring = [normed]
+        for hop in range(3):
+            ring.append(lax.ppermute(ring[-1], "sp", [(dev, (dev + 1) % 4) for dev in range(4)]))
+        gathered = jnp.roll(
+            jnp.concatenate(ring[::-1], axis=0),
+            (lax.axis_index("sp") + 1) * ring[0].shape[0],
+            axis=0,
+        )
         attention, activity, keys, values = mix(
             gathered, patch_id, keys, values, qkv_weight, norm_gain, inner_weight
         )

time: 169 us -> 178 us (1.053)
  waiting for transfers between devices: 54 us -> 74 us
  blocking collectives: 14.3 us -> 0 us
  other arithmetic: 21.6 us -> 24.3 us
    ppermute x0 -> x6, waiting for transfers between devices: none -> 18.6 us  [shards(): lax.ppermute(ring[-1], 'sp', [(dev, (dev + 1) % 4) for dev in range(4)])]
    all_gather x2 -> x0, blocking collectives: 14.3 us -> none  [shards(): gathered = lax.all_gather(normed, 'sp', axis=0, tiled=True)]
    concatenate x0 -> x2, other arithmetic: none -> 3.39 us  [shards(): jnp.roll(jnp.concatenate(ring[::-1], axis=0), (lax.axis_index('sp') + 1)...]
  transfers between devices with their start and end apart: 4 -> 10, of which waited for: 4 -> 10; matrix products, arithmetic and copies ran while one was open for 1% -> 4% of each run, Pallas kernels for 0% -> 0%
where the time goes in v1:
time: 178 us; the launch traced here: 177 us
  waiting for transfers between devices  74 us (42%)
  matrix products  44.3 us (25%)
  other arithmetic  24.3 us (14%)
  between operations  16.9 us (9%)
  local copies, waits for them, and re-layouts  13.4 us (8%)
  starting transfers between devices  4.4 us (2%)
    reduce_scatter x2, waiting for transfers between devices, shards(): lax.psum_scatter(jnp.dot(attention, attention_weight, preferred_element_t...  46 us
    dot_general x2, matrix products, shards(): jnp.dot(activity, outer_weight, preferred_element_type=jnp.float32)  21.6 us
    ppermute x6, waiting for transfers between devices, shards(): lax.ppermute(ring[-1], 'sp', [(dev, (dev + 1) % 4) for dev in range(4)])  18.6 us
    dot_general x2, matrix products, mix(): jnp.einsum('rd,dce->rce', normed, qkv_weight, preferred_element_type=jnp....  10.8 us
    ppermute x2, waiting for transfers between devices, shifted_2(): lax.ppermute(x, axis, [(i, (i + by) % length) for i in range(length)])  9.39 us
    dot_general x2, matrix products, shards(): jnp.dot(attention, attention_weight, preferred_element_type=jnp.float32)  5.36 us
    dot_general x2, matrix products, mix(): jnp.einsum('hrt,thd->rhd', weights, value_heads, preferred_element_type=j...  3.95 us
    unnamed x17, local copies, waits for them, and re-layouts  3.74 us
  transfers between devices with their start and end apart: 10, of which 10 were waited for; matrix products, arithmetic and copies ran while one was open for 4% of the time, Pallas kernels for 0%

profile of v1, /device:TPU:0, one launch (start us, length us, event | category | flops | bytes accessed | tf_op | source)
XLA Modules:
  0.0 177.4 jit_solution(11602473833291203638)
XLA Ops:
  7.2 1.5 fusion.134
  12.2 1.1 fusion.92
  14.9 2.3 %slice_bitcast_fusion = (bf16[512,512]{1,0:T(8,128)(2,1)}, bf16[512,512]{1,0:T(8,128)(2,1)}) fusion(bf16[1,2,512,512]{3,2,1,0:T(8,128)(2,1)} %param.21), kind=kLoop, calls=%fused_computation.59 | loop fusion | bytes 2097152 | tf_op jit(solution)/shard_map/squeeze | solution.py:93
  17.2 2.0 %collective-permute-done = bf16[16,3072]{1,0:T(8,128)(2,1)S(1)} collective-permute-done((bf16[16,3072]{1,0:T(8,128)(2,1)S(1)}, bf16[16,3072]{1,0:T(8,128)(2,1)S(1)}, u32[]{:S(2)}, u32[]{:S(2)}) %collective-permute-start) | collective-permute-done | bytes 98336 | tf_op jit(solution)/shard_map/ppermute | solution.py:103
  19.8 1.3 bitcast_convert_fusion.1
  21.1 2.1 %collective-permute-done.1 = bf16[16,3072]{1,0:T(8,128)(2,1)S(1)} collective-permute-done((bf16[16,3072]{1,0:T(8,128)(2,1)S(1)}, bf16[16,3072]{1,0:T(8,128)(2,1)S(1)}, u32[]{:S(2)}, u32[]{:S(2)}) %collective-permute-start.1) | collective-permute-done | bytes 98336 | tf_op jit(solution)/shard_map/ppermute | solution.py:103
  24.4 2.9 %collective-permute-done.2 = bf16[16,3072]{1,0:T(8,128)(2,1)} collective-permute-done((bf16[16,3072]{1,0:T(8,128)(2,1)S(1)}, bf16[16,3072]{1,0:T(8,128)(2,1)}, u32[]{:S(2)}, u32[]{:S(2)}) %collective-permute-start.2) | collective-permute-done | bytes 98336 | tf_op jit(solution)/shard_map/ppermute | solution.py:103
  27.3 1.7 fusion.74
  29.8 5.4 %fusion.20 = bf16[64,3,512]{2,0,1:T(8,128)(2,1)S(1)} fusion(bf16[1,3072,3,512]{3,1,2,0:T(8,128)(2,1)} %param.16, bf16[64,3072]{1,0:T(8,128)(2,1)S(1)} %fusion.74), kind=kOutput, calls=%fused_computation.24 | convolution fusion | flops 604078080 | bytes 10027008 | tf_op jit(solution)/shard_map/rd,dce->rce/dot_general | solution.py:46
  41.0 1.3 fusion.113
  42.4 1.3 convolution_multiply_fusion.1
  44.7 2.0 %fusion.26 = bf16[4,8,8,128]{3,2,1,0:T(8,128)(2,1)S(1)} fusion(f32[4,64]{1,0:T(4,128)S(1)} %fusion.136, f32[4,64,512]{2,1,0:T(8,128)} %copy-done.3, bf16[512,512]{1,0:T(8,128)(2,1)} %get-tuple-element.10), kind=kOutput, calls=%fused_computation.28 | convolution fusion | flops 33981184 | bytes 1115136 | tf_op jit(solution)/shard_map/hrt,thd->rhd/dot_general | solution.py:63
  46.8 10.8 %fusion.4 = f32[64,3072]{1,0:T(8,128)} fusion(bf16[1,1536,3072]{2,1,0:T(8,128)(2,1)} %param.20, bf16[64,3072]{1,0:T(8,128)(2,1)} %copy-done.1, bf16[1,3072,1536]{2,1,0:T(8,128)(2,1)} %param.18), kind=kOutput, calls=%fused_computation.4 | convolution fusion | flops 1208844288 | bytes 20054016 | tf_op jit(solution)/shard_map/dot_general | solution.py:114
  57.6 2.7 %convolution_add_fusion.1 = f32[64,3072]{1,0:T(8,128)} fusion(f32[64,3072]{1,0:T(8,128)} %fusion.4, bf16[1,512,3072]{2,1,0:T(8,128)(2,1)S(1)} %copy-done, bf16[4,8,8,128]{3,2,1,0:T(8,128)(2,1)S(1)} %fusion.26), kind=kOutput, calls=%fused_computation.15 | convolution fusion | flops 201523200 | bytes 4784128 | tf_op jit(solution)/shard_map/dot_general | solution.py:113
  60.3 25.4 %reduce-scatter.3.cloned.1.call-done = f32[16,3072]{1,0:T(8,128)} async-done(((f32[64,3072]{1,0:T(8,128)}), f32[16,3072]{1,0:T(8,128)}) %reduce-scatter.3.cloned.1.call-update) | async-done | bytes 196624 | tf_op jit(solution)/shard_map/reduce_scatter | solution.py:112
  86.6 1.5 collective-permute-start.3
  88.2 5.8 %collective-permute-done.3 = bf16[16,3072]{1,0:T(8,128)(2,1)S(1)} collective-permute-done((bf16[16,3072]{1,0:T(8,128)(2,1)S(1)}, bf16[16,3072]{1,0:T(8,128)(2,1)S(1)}, u32[]{:S(2)}, u32[]{:S(2)}) %collective-permute-start.3) | collective-permute-done | bytes 98336 | tf_op jit(solution)/shard_map/ppermute | solution.py:13
  94.6 4.0 %collective-permute-done.4 = bf16[16,3072]{1,0:T(8,128)(2,1)S(1)} collective-permute-done((bf16[16,3072]{1,0:T(8,128)(2,1)S(1)}, bf16[16,3072]{1,0:T(8,128)(2,1)S(1)}, u32[]{:S(2)}, u32[]{:S(2)}) %collective-permute-start.4) | collective-permute-done | bytes 98336 | tf_op jit(solution)/shard_map/ppermute | solution.py:103
  98.6 4.0 %collective-permute-done.5 = bf16[16,3072]{1,0:T(8,128)(2,1)S(1)} collective-permute-done((bf16[16,3072]{1,0:T(8,128)(2,1)S(1)}, bf16[16,3072]{1,0:T(8,128)(2,1)S(1)}, u32[]{:S(2)}, u32[]{:S(2)}) %collective-permute-start.5) | collective-permute-done | bytes 98336 | tf_op jit(solution)/shard_map/ppermute | solution.py:103
  103.3 3.5 %collective-permute-done.6 = bf16[16,3072]{1,0:T(8,128)(2,1)} collective-permute-done((bf16[16,3072]{1,0:T(8,128)(2,1)S(1)}, bf16[16,3072]{1,0:T(8,128)(2,1)}, u32[]{:S(2)}, u32[]{:S(2)}) %collective-permute-start.6) | collective-permute-done | bytes 98336 | tf_op jit(solution)/shard_map/ppermute | solution.py:103
  106.8 1.7 fusion.67
  109.2 5.4 %fusion.23 = bf16[64,3,512]{2,0,1:T(8,128)(2,1)S(1)} fusion(bf16[1,3072,3,512]{3,1,2,0:T(8,128)(2,1)} %param.16, bf16[64,3072]{1,0:T(8,128)(2,1)S(1)} %fusion.67), kind=kOutput, calls=%fused_computation.25 | convolution fusion | flops 604078080 | bytes 10027008 | tf_op jit(solution)/shard_map/rd,dce->rce/dot_general | solution.py:46
  116.0 10.8 %fusion.2 = f32[64,3072]{1,0:T(8,128)} fusion(bf16[1,1536,3072]{2,1,0:T(8,128)(2,1)} %param.20, bf16[64,3072]{1,0:T(8,128)(2,1)} %copy-done.2, bf16[1,3072,1536]{2,1,0:T(8,128)(2,1)} %param.18), kind=kOutput, calls=%fused_computation.2 | convolution fusion | flops 1208844288 | bytes 20054016 | tf_op jit(solution)/shard_map/dot_general | solution.py:114
  126.7 1.6 mul.275
  129.4 1.6 reshape.151
  133.9 1.3 convolution_multiply_fusion
  136.3 1.9 %fusion.27 = bf16[4,8,8,128]{3,2,1,0:T(8,128)(2,1)S(1)} fusion(f32[4,64]{1,0:T(4,128)S(1)} %fusion.137, f32[4,64,512]{2,1,0:T(8,128)} %copy-done.4, bf16[512,512]{1,0:T(8,128)(2,1)} %get-tuple-element.8), kind=kOutput, calls=%fused_computation.29 | convolution fusion | flops 33981184 | bytes 1115136 | tf_op jit(solution)/shard_map/hrt,thd->rhd/dot_general | solution.py:63
  138.3 2.7 %convolution_add_fusion = f32[64,3072]{1,0:T(8,128)} fusion(f32[64,3072]{1,0:T(8,128)} %fusion.2, bf16[1,512,3072]{2,1,0:T(8,128)(2,1)S(1)} %copy-done, bf16[4,8,8,128]{3,2,1,0:T(8,128)(2,1)S(1)} %fusion.27), kind=kOutput, calls=%fused_computation.14 | convolution fusion | flops 201523200 | bytes 4784128 | tf_op jit(solution)/shard_map/dot_general | solution.py:113
  141.0 20.7 %reduce-scatter.5.cloned.1.call-done = f32[16,3072]{1,0:T(8,128)} async-done(((f32[64,3072]{1,0:T(8,128)}), f32[16,3072]{1,0:T(8,128)}) %reduce-scatter.5.cloned.1.call-update) | async-done | bytes 196624 | tf_op jit(solution)/shard_map/reduce_scatter | solution.py:112
  162.6 1.5 collective-permute-start.7
  164.1 2.3 %maximum_bitcast_fusion = bf16[1,2,512,512]{3,2,1,0:T(8,128)(2,1)} fusion(bf16[1,512,512]{2,1,0:T(8,128)(2,1)} %bitcast.182, bf16[1,512,512]{2,1,0:T(8,128)(2,1)} %bitcast.181), kind=kLoop, calls=%fused_computation.30 | loop fusion | flops 524288 | bytes 2097152 | tf_op jit(solution)/shard_map/broadcast_in_dim | solution.py:121
  166.4 3.6 %collective-permute-done.7 = bf16[16,3072]{1,0:T(8,128)(2,1)S(1)} collective-permute-done((bf16[16,3072]{1,0:T(8,128)(2,1)S(1)}, bf16[16,3072]{1,0:T(8,128)(2,1)S(1)}, u32[]{:S(2)}, u32[]{:S(2)}) %collective-permute-start.7) | collective-permute-done | bytes 98336 | tf_op jit(solution)/shard_map/ppermute | solution.py:13
  (63 shorter events, 22.8 us)
Async XLA Ops:
  7.2 50.4 %copy-start = (bf16[1,512,3072]{2,1,0:T(8,128)(2,1)S(1)}, bf16[1,512,3072]{2,1,0:T(8,128)(2,1)}, u32[]{:S(2)}) copy-start(bf16[1,512,3072]{2,1,0:T(8,128)(2,1)} %param.19) | copy-start | bytes 9437188
  7.2 78.5 %reduce-scatter.3.cloned.1.call-start = ((), (), s32[]{:S(2)}) async-start(), calls=%async_computation.2 | async-start | bytes 983040 | tf_op jit(solution)/shard_map/reduce_scatter | solution.py:112
  14.4 4.8 %collective-permute-start = (bf16[16,3072]{1,0:T(8,128)(2,1)S(1)}, bf16[16,3072]{1,0:T(8,128)(2,1)S(1)}, u32[]{:S(2)}, u32[]{:S(2)}) collective-permute-start(bf16[16,3072]{1,0:T(8,128)(2,1)S(1)} %fusion.95), channel_id=1, source_target_pairs={{0,1},{1,2},{2,3},{3,0},{4,5},{5,6},{6,7},{7,4},{8,9},{9,10},{10,1... | collective-permute-start | bytes 294920 | tf_op jit(solution)/shard_map/ppermute | solution.py:103
  19.1 4.0 %collective-permute-start.1 = (bf16[16,3072]{1,0:T(8,128)(2,1)S(1)}, bf16[16,3072]{1,0:T(8,128)(2,1)S(1)}, u32[]{:S(2)}, u32[]{:S(2)}) collective-permute-start(bf16[16,3072]{1,0:T(8,128)(2,1)S(1)} %collective-permute-done), channel_id=1, source_target_pairs={{0,1},{1,2},{2,3},{3,0},{4,5},{5,6},{6,7},{7,4},{8,9},{9,10},{10,1... | collective-permute-start | bytes 294920 | tf_op jit(solution)/shard_map/ppermute | solution.py:103
  23.2 4.1 %collective-permute-start.2 = (bf16[16,3072]{1,0:T(8,128)(2,1)S(1)}, bf16[16,3072]{1,0:T(8,128)(2,1)}, u32[]{:S(2)}, u32[]{:S(2)}) collective-permute-start(bf16[16,3072]{1,0:T(8,128)(2,1)S(1)} %collective-permute-done.1), channel_id=1, source_target_pairs={{0,1},{1,2},{2,3},{3,0},{4,5},{5,6},{6,7},{7,4},{8,9},{9,10},{10,1... | collective-permute-start | bytes 294920 | tf_op jit(solution)/shard_map/ppermute | solution.py:103
  29.0 0.7 copy-start.1
  43.7 0.8 copy-start.3
  46.8 38.9 %copy-start.5 = (bf16[1,16,3072]{2,1,0:T(8,128)(2,1)S(1)}, bf16[1,16,3072]{2,1,0:T(8,128)(2,1)}, u32[]{:S(2)}) copy-start(bf16[1,16,3072]{2,1,0:T(8,128)(2,1)} %param.12) | copy-start | bytes 294916
  60.3 101.4 %reduce-scatter.5.cloned.1.call-start = ((), (), s32[]{:S(2)}) async-start(), calls=%async_computation.3 | async-start | bytes 983040 | tf_op jit(solution)/shard_map/reduce_scatter | solution.py:112
  86.6 7.4 %collective-permute-start.3 = (bf16[16,3072]{1,0:T(8,128)(2,1)S(1)}, bf16[16,3072]{1,0:T(8,128)(2,1)S(1)}, u32[]{:S(2)}, u32[]{:S(2)}) collective-permute-start(bf16[16,3072]{1,0:T(8,128)(2,1)S(1)} %fusion.96), channel_id=1, source_target_pairs={{0,4},{4,8},{8,12},{12,16},{16,20},{20,24},{24,28},{28,0},{1,5},{5... | collective-permute-start | bytes 294920 | tf_op jit(solution)/shard_map/ppermute | solution.py:13
  94.5 4.1 %collective-permute-start.4 = (bf16[16,3072]{1,0:T(8,128)(2,1)S(1)}, bf16[16,3072]{1,0:T(8,128)(2,1)S(1)}, u32[]{:S(2)}, u32[]{:S(2)}) collective-permute-start(bf16[16,3072]{1,0:T(8,128)(2,1)S(1)} %fusion.91), channel_id=1, source_target_pairs={{0,1},{1,2},{2,3},{3,0},{4,5},{5,6},{6,7},{7,4},{8,9},{9,10},{10,1... | collective-permute-start | bytes 294920 | tf_op jit(solution)/shard_map/ppermute | solution.py:103
  98.6 4.0 %collective-permute-start.5 = (bf16[16,3072]{1,0:T(8,128)(2,1)S(1)}, bf16[16,3072]{1,0:T(8,128)(2,1)S(1)}, u32[]{:S(2)}, u32[]{:S(2)}) collective-permute-start(bf16[16,3072]{1,0:T(8,128)(2,1)S(1)} %collective-permute-done.4), channel_id=1, source_target_pairs={{0,1},{1,2},{2,3},{3,0},{4,5},{5,6},{6,7},{7,4},{8,9},{9,10},{10,1... | collective-permute-start | bytes 294920 | tf_op jit(solution)/shard_map/ppermute | solution.py:103
  102.6 4.1 %collective-permute-start.6 = (bf16[16,3072]{1,0:T(8,128)(2,1)S(1)}, bf16[16,3072]{1,0:T(8,128)(2,1)}, u32[]{:S(2)}, u32[]{:S(2)}) collective-permute-start(bf16[16,3072]{1,0:T(8,128)(2,1)S(1)} %collective-permute-done.5), channel_id=1, source_target_pairs={{0,1},{1,2},{2,3},{3,0},{4,5},{5,6},{6,7},{7,4},{8,9},{9,10},{10,1... | collective-permute-start | bytes 294920 | tf_op jit(solution)/shard_map/ppermute | solution.py:103
  108.5 0.7 copy-start.2
  115.9 16.1 %copy-start.7 = (f32[128]{0:T(128)S(1)}, f32[128]{0:T(128)}, u32[]{:S(2)}) copy-start(f32[128]{0:T(128)} %get-tuple-element.21) | copy-start | bytes 1540
  116.0 17.3 %copy-start.6 = (f32[512]{0:T(512)S(1)}, f32[512]{0:T(512)}, u32[]{:S(2)}) copy-start(f32[512]{0:T(512)} %broadcast_bitcast_fusion) | copy-start | bytes 6148
  135.3 0.8 copy-start.4
  162.6 7.4 %collective-permute-start.7 = (bf16[16,3072]{1,0:T(8,128)(2,1)S(1)}, bf16[16,3072]{1,0:T(8,128)(2,1)S(1)}, u32[]{:S(2)}, u32[]{:S(2)}) collective-permute-start(bf16[16,3072]{1,0:T(8,128)(2,1)S(1)} %fusion.97), channel_id=1, source_target_pairs={{0,4},{4,8},{8,12},{12,16},{16,20},{20,24},{24,28},{28,0},{1,5},{5... | collective-permute-start | bytes 294920 | tf_op jit(solution)/shard_map/ppermute | solution.py:13
Sparse Core Ops, SparseCore 0:
  60.4 25.2 reduce-scatter.2
  141.1 20.5 reduce-scatter.4
